TPU v7x, 128 devices: a whole 4x4x4 slice. The times are simulated.
128 devices in a mesh: pts: 32 (over z, x, core), rep: 4 (over y).
Axes of the slice: x: 4, y: 4, z: 4, core: 2. Of those that a mesh axis runs over, the one named last changes fastest.
Arguments:
- target_xyz: float32 [3, 32768], P(None, 'pts'), may hold values from 0 to 1
- source_xyz: float32 [3, 65536], P(None, ('pts', 'rep')), may hold values from 0 to 1
- target_count: int32 [32], P('pts'), may hold values from 1 to 1024, as said below
- source_count: int32 [128], P(('pts', 'rep')), may hold values from 1 to 512, as said below
- psi: bfloat16 [32768, 256], P('pts'), may hold values from -6 to 6
- omega: bfloat16 [65536, 256], P(('pts', 'rep')), may hold values from -6 to 6
Outputs:
- range_sketch: float32 [32768, 256], P('pts')
- corange_sketch: float32 [65536, 256], P(('pts', 'rep'))
- core: float32 [256, 256], replicated
- range_gram: float32 [256, 256], replicated
- corange_gram: float32 [256, 256], replicated
Inputs may be any that keep to these rules, and one draw needn't show every extreme that they name: `target_count`: each group holds 1 to 1024 live targets; some group holds exactly 1024. `source_count`: each shard holds 1 to 512 live sources; some shard holds exactly 512.
All inputs are finite; a program needn't handle non-finite values.
Results may differ from a plain program's by a relative error of at most 0.0003.
The roundings to bfloat16 on the way count: a program that leaves them out, or rounds other values in their place, can miss the bound.
Values may be sent and summed in bfloat16 or wider, within the bound.
No kernel may reach another device: no remote copies, remote signals or barrier semaphores. Data moves between devices by JAX's collectives and lax.ppermute only.
A program may use at most 64 MiB of HBM per device.

v0:
```python
import math
import jax
import jax.numpy as jnp
from jax import lax
from jax.sharding import PartitionSpec as P

SHIFT = 1.05
SPREAD = 8.0


def tile_block(tgt, src):
    dx = tgt[0][:, None] - (src[0][None, :] + SHIFT)
    dy = SPREAD * (tgt[1][:, None] - src[1][None, :])
    dz = SPREAD * (tgt[2][:, None] - src[2][None, :])
    return lax.rsqrt(dx * dx + dy * dy + dz * dz).astype(jnp.bfloat16)


def local(target_xyz, source_xyz, target_count, source_count, psi, omega):
    tcap = psi.shape[0]
    scap = omega.shape[0]
    width = psi.shape[1]
    n_pts = lax.axis_size("pts")
    n_rep = lax.axis_size("rep")
    all_targets = tcap * n_pts
    all_sources = scap * n_pts * n_rep
    tlive = jnp.arange(tcap, dtype=jnp.int32) < target_count[0]
    slive = jnp.arange(scap, dtype=jnp.int32) < source_count[0]
    psi_live = jnp.where(tlive[:, None], psi, jnp.zeros_like(psi))
    omega_live = jnp.where(slive[:, None], omega, jnp.zeros_like(omega))
    hi = lax.Precision.HIGHEST
    src_all = lax.all_gather(source_xyz, "pts", axis=1, tiled=True)
    piece = lax.all_gather(omega_live, "pts", axis=0, tiled=True)

    def range_inner(j, acc):
        rows = lax.dynamic_slice_in_dim(piece, j * scap, scap, 0)
        where = lax.dynamic_slice_in_dim(src_all, j * scap, scap, 1)
        return acc + jnp.dot(
            tile_block(target_xyz, where), rows, preferred_element_type=jnp.float32
        )

    y_part = lax.fori_loop(
        0, piece.shape[0] // scap, range_inner, jnp.zeros((tcap, width), jnp.float32)
    )
    y_sum = lax.psum(y_part, "rep") * (2.0 / math.sqrt(all_sources))
    range_sketch = jnp.where(tlive[:, None], y_sum, jnp.zeros_like(y_sum))
    tgt_all = lax.all_gather(target_xyz, "pts", axis=1, tiled=True)
    corange_piece = lax.all_gather(psi_live, "pts", axis=0, tiled=True)

    def corange_inner(j, acc):
        rows = lax.dynamic_slice_in_dim(corange_piece, j * tcap, tcap, 0)
        where = lax.dynamic_slice_in_dim(tgt_all, j * tcap, tcap, 1)
        tile = tile_block(where, source_xyz)
        return acc + lax.dot_general(
            tile, rows, (((0,), (0,)), ((), ())), preferred_element_type=jnp.float32
        )

    z_sum = lax.fori_loop(
        0, corange_piece.shape[0] // tcap, corange_inner, jnp.zeros((scap, width), jnp.float32)
    )
    z_scaled = z_sum * (2.0 / math.sqrt(all_targets))
    corange_sketch = jnp.where(slive[:, None], z_scaled, jnp.zeros_like(z_scaled))
    z_gram_part = jnp.dot(corange_sketch.T, corange_sketch, precision=hi)
    core_part = jnp.dot(psi_live.astype(jnp.float32).T, range_sketch, precision=hi)
    y_gram_part = jnp.dot(range_sketch.T, range_sketch, precision=hi)
    core_sum, y_gram = lax.psum((core_part, y_gram_part), "pts")
    z_gram = lax.psum(z_gram_part, ("pts", "rep"))
    core = core_sum / math.sqrt(all_targets)
    range_gram = y_gram / all_targets
    corange_gram = z_gram / all_sources
    return (range_sketch, corange_sketch, core, range_gram, corange_gram)


def solution(mesh):
    return jax.shard_map(
        local,
        mesh=mesh,
        in_specs=(
            P(None, "pts"),
            P(None, ("pts", "rep")),
            P("pts"),
            P(("pts", "rep")),
            P("pts", None),
            P(("pts", "rep"), None),
        ),
        out_specs=(P("pts", None), P(("pts", "rep"), None), P(), P(), P()),
        check_vma=False,
    )
```

profile of v0, /device:TPU:1, one launch (start us, length us, event | category | flops | bytes accessed | tf_op | source)
XLA Modules:
  0.0 550.0 jit_solution(14603858195827019406)
XLA Ops:
  9.7 27.6 %all_gather.12 = f32[3,16384]{1,0:T(4,128)S(1)} all-gather(f32[3,512]{1,0:T(4,128)} %param.11), channel_id=1, replica_groups=mesh['pts'=32,'rep'=4] {'pts'}, dimensions={1}, use_global_device_ids=true | all-gather | bytes 202752 | tf_op jit(solution)/shard_map/all_gather | solution.py:31
  37.3 30.2 %all-gather.3.cloned.1.call-done = bf16[16384,256]{1,0:T(8,128)(2,1)} async-done(((bf16[512,256]{1,0:T(8,128)(2,1)}), bf16[16384,256]{1,0:T(8,128)(2,1)}) %all-gather.3.cloned.1.call-update) | async-done | bytes 8388624 | tf_op jit(solution)/shard_map/all_gather | solution.py:32
  67.5 96.4 %while.28 = (s32[]{:T(128)}, f32[1024,256]{1,0:T(8,128)S(1)}, f32[3,1024]{1,0:T(4,128)}, f32[3,16384]{1,0:T(4,128)S(1)}, bf16[16384,256]{1,0:T(8,128)(2,1)}, /*i...) while((s32[]{:T(128)}, f32[1024,256]{1,0:T(8,128)S(1)}, ...), condition=%wide.region_1.2_spmd.clone, body=%wide.region_0.1_spmd.clone.sunk | while | flops 274727424 | bytes 2414797 | solution.py:41
  166.7 24.7 %all_gather.14 = f32[3,32768]{1,0:T(4,128)S(1)} all-gather(f32[3,1024]{1,0:T(4,128)S(1)} %copy-done.5), channel_id=1, replica_groups=mesh['pts'=32,'rep'=4] {'pts'}, dimensions={1}, use_global_device_ids=true | all-gather | bytes 405504 | tf_op jit(solution)/shard_map/all_gather | solution.py:46
  191.4 17.0 %all-reduce.5.cloned.1.call-done = f32[1024,256]{1,0:T(8,128)} async-done(((f32[1024,256]{1,0:T(8,128)}), f32[1024,256]{1,0:T(8,128)}) %all-reduce.5.cloned.1.call-update) | async-done | bytes 1048592 | tf_op jit(solution)/shard_map/psum | solution.py:44
  211.4 2.6 fusion.22
  214.0 73.1 %all-gather.5.cloned.1.call-done = bf16[32768,256]{1,0:T(8,128)(2,1)} async-done(((bf16[1024,256]{1,0:T(8,128)(2,1)}), bf16[32768,256]{1,0:T(8,128)(2,1)}) %all-gather.5.cloned.1.call-update) | async-done | bytes 16777232 | tf_op jit(solution)/shard_map/all_gather | solution.py:47
  287.1 81.4 %while.29 = (s32[]{:T(128)}, f32[512,256]{1,0:T(8,128)S(1)}, f32[3,32768]{1,0:T(4,128)S(1)}, f32[3,512]{1,0:T(4,128)S(1)}, bf16[32768,256]{1,0:T(8,128)(2,1)}, /...) while((s32[]{:T(128)}, f32[512,256]{1,0:T(8,128)S(1)}, ...), condition=%wide.region_4.5_spmd.clone, body=%wide.region_3.4_spmd.clone.sunk | while | flops 274465280 | bytes 1628365 | solution.py:57
  287.2 2.4 convolution_add_fusion.5
  289.8 2.4 convolution_add_fusion.5
  292.3 2.4 convolution_add_fusion.5
  294.8 2.4 convolution_add_fusion.5
  297.4 2.4 convolution_add_fusion.5
  300.0 2.4 convolution_add_fusion.5
  302.5 2.4 convolution_add_fusion.5
  305.0 2.4 convolution_add_fusion.5
  315.2 2.4 convolution_add_fusion.5
  317.8 2.4 convolution_add_fusion.5
  320.3 2.4 convolution_add_fusion.5
  322.9 2.4 convolution_add_fusion.5
  325.4 2.4 convolution_add_fusion.5
  327.9 2.4 convolution_add_fusion.5
  333.0 2.4 convolution_add_fusion.5
  335.6 2.4 convolution_add_fusion.5
  338.1 2.4 convolution_add_fusion.5
  348.3 2.4 convolution_add_fusion.5
  350.9 2.4 convolution_add_fusion.5
  355.9 2.4 convolution_add_fusion.5
  358.5 2.4 convolution_add_fusion.5
  361.0 2.4 convolution_add_fusion.5
  370.5 24.1 %all-reduce.9.cloned.1.call-done = (f32[256,256]{1,0:T(8,128)}, f32[256,256]{1,0:T(8,128)}) async-done(((f32[256,256]{1,0:T(8,128)}, f32[256,256]{1,0:T(8,128)}), (f32[256,256]{1,0:T(8,128)}, f32[256,256]{1,0:T(8,128)})) %all-reduce.9.cloned.1.call-update) | async-done | bytes 524304 | tf_op jit(solution)/shard_map/psum | solution.py:65
  396.4 145.4 %all-reduce.7.cloned.1.call-done = f32[256,256]{1,0:T(8,128)} async-done(((f32[256,256]{1,0:T(8,128)}), f32[256,256]{1,0:T(8,128)}) %all-reduce.7.cloned.1.call-update) | async-done | bytes 262160 | tf_op jit(solution)/shard_map/psum | solution.py:66
  (206 shorter events, 134.8 us)
Async XLA Ops:
  7.2 60.3 %all-gather.3.cloned.1.call-start = ((), (), s32[]{:S(2)}) async-start(), calls=%async_computation | async-start | bytes 8650752 | tf_op jit(solution)/shard_map/all_gather | solution.py:32
  9.7 198.7 %all-reduce.5.cloned.1.call-start = ((), (), s32[]{:S(2)}) async-start(), calls=%async_computation.1 | async-start | bytes 2097152 | tf_op jit(solution)/shard_map/psum | solution.py:44
  67.5 98.1 %copy-start.4 = (bf16[1024,256]{1,0:T(8,128)(2,1)S(1)}, bf16[1024,256]{1,0:T(8,128)(2,1)}, u32[]{:S(2)}) copy-start(bf16[1024,256]{1,0:T(8,128)(2,1)} %param.14) | copy-start | bytes 1572868
  163.9 1.0 copy-start.3
  163.9 2.8 copy-start.5
  164.9 122.2 %all-gather.5.cloned.1.call-start = ((), (), s32[]{:S(2)}) async-start(), calls=%async_computation.2 | async-start | bytes 17301504 | tf_op jit(solution)/shard_map/all_gather | solution.py:47
  166.6 43.2 %copy-start.2 = (bf16[1024,256]{1,0:T(8,128)(2,1)S(1)}, bf16[1024,256]{1,0:T(8,128)(2,1)}, u32[]{:S(2)}) copy-start(bf16[1024,256]{1,0:T(8,128)(2,1)} %broadcast_select_fusion) | copy-start | bytes 1572868
  166.6 227.9 %all-reduce.9.cloned.1.call-start = ((), (), s32[]{:S(2)}) async-start(), calls=%async_computation.4 | async-start | bytes 1048576 | tf_op jit(solution)/shard_map/psum | solution.py:65
  209.8 4.1 copy-start
  209.9 77.3 %copy-start.6 = (f32[3,512]{1,0:T(4,128)S(1)}, f32[3,512]{1,0:T(4,128)}, u32[]{:S(2)}) copy-start(f32[3,512]{1,0:T(4,128)} %param.11) | copy-start | bytes 18436
  214.0 327.8 %all-reduce.7.cloned.1.call-start = ((), (), s32[]{:S(2)}) async-start(), calls=%async_computation.3 | async-start | bytes 524288 | tf_op jit(solution)/shard_map/psum | solution.py:66
  368.7 174.8 %copy-start.1 = (f32[512,256]{1,0:T(8,128)}, f32[512,256]{1,0:T(8,128)S(1)}, u32[]{:S(2)}) copy-start(f32[512,256]{1,0:T(8,128)S(1)} %multiply_select_fusion.1) | copy-start | bytes 1572868
Sparse Core Ops, SparseCore 0:
  10.8 56.6 all-gather.2
  165.0 43.3 all-reduce.4
  211.2 75.8 all-gather.4
  290.8 103.6 all-reduce.8
  399.1 142.5 all-reduce.6
where the time goes:
time: 555 us; the launch traced here: 550 us
  waiting for transfers between devices  290 us (52%)
  matrix products  148 us (27%)
  blocking collectives  52.2 us (9%)
  local copies, waits for them, and re-layouts  30.9 us (6%)
  between operations  15.2 us (3%)
  other arithmetic  10.8 us (2%)
    psum x1, waiting for transfers between devices, local(): z_gram = lax.psum(z_gram_part, ('pts', 'rep'))  145 us
    dot_general x32, matrix products, corange_inner(): lax.dot_general(tile, rows, (((0,), (0,)), ((), ())), preferred_element_t...  76.9 us
    all_gather x1, waiting for transfers between devices, local(): corange_piece = lax.all_gather(psi_live, 'pts', axis=0, tiled=True)  73.1 us
    dot_general x32, matrix products, range_inner(): jnp.dot(tile_block(target_xyz, where), rows, preferred_element_type=jnp.f...  65.5 us
    all_gather x1, waiting for transfers between devices, local(): piece = lax.all_gather(omega_live, 'pts', axis=0, tiled=True)  30.2 us
    slice x64, local copies, waits for them, and re-layouts, tile_block(): dx = tgt[0][:, None] - (src[0][None, :] + SHIFT)  30 us
    all_gather x1, blocking collectives, local(): src_all = lax.all_gather(source_xyz, 'pts', axis=1, tiled=True)  27.6 us
    all_gather x1, blocking collectives, local(): tgt_all = lax.all_gather(target_xyz, 'pts', axis=1, tiled=True)  24.7 us
  transfers between devices with their start and end apart: 5, of which 5 were waited for; matrix products, arithmetic and copies ran while one was open for 16% of the time, Pallas kernels for 0%

commit v1 on v0

--- a/solution.py
+++ b/solution.py
@@ -63,7 +63,7 @@
     core_part = jnp.dot(psi_live.astype(jnp.float32).T, range_sketch, precision=hi)
     y_gram_part = jnp.dot(range_sketch.T, range_sketch, precision=hi)
     core_sum, y_gram = lax.psum((core_part, y_gram_part), "pts")
-    z_gram = lax.psum(z_gram_part, ("pts", "rep"))
+    z_gram = jnp.sum(lax.all_gather(z_gram_part, ("pts", "rep")), axis=0)
     core = core_sum / math.sqrt(all_targets)
     range_gram = y_gram / all_targets
     corange_gram = z_gram / all_sources

time: 555 us -> 528 us (0.951)
  waiting for transfers between devices: 290 us -> 252 us
  other arithmetic: 10.8 us -> 21.9 us
    psum x1 -> x0, waiting for transfers between devices: 145 us -> none  [local(): z_gram = lax.psum(z_gram_part, ('pts', 'rep'))]
    all_gather x0 -> x1, waiting for transfers between devices: none -> 107 us  [local(): z_gram = jnp.sum(lax.all_gather(z_gram_part, ('pts', 'rep')), axis=0)]
    reduce_sum x0 -> x1, other arithmetic: none -> 12 us  [local(): z_gram = jnp.sum(lax.all_gather(z_gram_part, ('pts', 'rep')), axis=0)]
  transfers between devices with their start and end apart: 5 -> 5, of which waited for: 5 -> 5; matrix products, arithmetic and copies ran while one was open for 16% -> 17% of each run, Pallas kernels for 0% -> 0%
where the time goes in v1:
time: 528 us; the launch traced here: 523 us
  waiting for transfers between devices  252 us (48%)
  matrix products  148 us (28%)
  blocking collectives  52.2 us (10%)
  local copies, waits for them, and re-layouts  30.9 us (6%)
  other arithmetic  21.9 us (4%)
  between operations  15.2 us (3%)
    all_gather x1, waiting for transfers between devices, local(): z_gram = jnp.sum(lax.all_gather(z_gram_part, ('pts', 'rep')), axis=0)  107 us
    dot_general x32, matrix products, corange_inner(): lax.dot_general(tile, rows, (((0,), (0,)), ((), ())), preferred_element_t...  76.9 us
    all_gather x1, waiting for transfers between devices, local(): corange_piece = lax.all_gather(psi_live, 'pts', axis=0, tiled=True)  73.1 us
    dot_general x32, matrix products, range_inner(): jnp.dot(tile_block(target_xyz, where), rows, preferred_element_type=jnp.f...  65.5 us
    all_gather x1, waiting for transfers between devices, local(): piece = lax.all_gather(omega_live, 'pts', axis=0, tiled=True)  30.2 us
    slice x64, local copies, waits for them, and re-layouts, tile_block(): dx = tgt[0][:, None] - (src[0][None, :] + SHIFT)  30 us
    all_gather x1, blocking collectives, local(): src_all = lax.all_gather(source_xyz, 'pts', axis=1, tiled=True)  27.6 us
    all_gather x1, blocking collectives, local(): tgt_all = lax.all_gather(target_xyz, 'pts', axis=1, tiled=True)  24.7 us
  transfers between devices with their start and end apart: 5, of which 5 were waited for; matrix products, arithmetic and copies ran while one was open for 17% of the time, Pallas kernels for 0%

profile of v1, /device:TPU:1, one launch (start us, length us, event | category | flops | bytes accessed | tf_op | source)
XLA Modules:
  0.0 523.1 jit_solution(4474977850387014837)
XLA Ops:
  9.7 27.6 %all_gather.18 = f32[3,16384]{1,0:T(4,128)S(1)} all-gather(f32[3,512]{1,0:T(4,128)} %param.11), channel_id=1, replica_groups=mesh['pts'=32,'rep'=4] {'pts'}, dimensions={1}, use_global_device_ids=true | all-gather | bytes 202752 | tf_op jit(solution)/shard_map/all_gather | solution.py:31
  37.3 30.2 %all-gather.5.cloned.1.call-done = bf16[16384,256]{1,0:T(8,128)(2,1)} async-done(((bf16[512,256]{1,0:T(8,128)(2,1)}), bf16[16384,256]{1,0:T(8,128)(2,1)}) %all-gather.5.cloned.1.call-update) | async-done | bytes 8388624 | tf_op jit(solution)/shard_map/all_gather | solution.py:32
  67.5 96.4 %while.28 = (s32[]{:T(128)}, f32[1024,256]{1,0:T(8,128)S(1)}, f32[3,1024]{1,0:T(4,128)}, f32[3,16384]{1,0:T(4,128)S(1)}, bf16[16384,256]{1,0:T(8,128)(2,1)}, /*i...) while((s32[]{:T(128)}, f32[1024,256]{1,0:T(8,128)S(1)}, ...), condition=%wide.region_1.2_spmd.clone, body=%wide.region_0.1_spmd.clone.sunk | while | flops 274727424 | bytes 2414797 | solution.py:41
  166.7 24.7 %all_gather.20 = f32[3,32768]{1,0:T(4,128)S(1)} all-gather(f32[3,1024]{1,0:T(4,128)S(1)} %copy-done.5), channel_id=1, replica_groups=mesh['pts'=32,'rep'=4] {'pts'}, dimensions={1}, use_global_device_ids=true | all-gather | bytes 405504 | tf_op jit(solution)/shard_map/all_gather | solution.py:46
  191.4 17.0 %all-reduce.4.cloned.1.call-done = f32[1024,256]{1,0:T(8,128)} async-done(((f32[1024,256]{1,0:T(8,128)}), f32[1024,256]{1,0:T(8,128)}) %all-reduce.4.cloned.1.call-update) | async-done | bytes 1048592 | tf_op jit(solution)/shard_map/psum | solution.py:44
  211.4 2.6 fusion.22
  214.0 73.1 %all-gather.7.cloned.1.call-done = bf16[32768,256]{1,0:T(8,128)(2,1)} async-done(((bf16[1024,256]{1,0:T(8,128)(2,1)}), bf16[32768,256]{1,0:T(8,128)(2,1)}) %all-gather.7.cloned.1.call-update) | async-done | bytes 16777232 | tf_op jit(solution)/shard_map/all_gather | solution.py:47
  287.1 81.4 %while.29 = (s32[]{:T(128)}, f32[512,256]{1,0:T(8,128)S(1)}, f32[3,32768]{1,0:T(4,128)S(1)}, f32[3,512]{1,0:T(4,128)S(1)}, bf16[32768,256]{1,0:T(8,128)(2,1)}, /...) while((s32[]{:T(128)}, f32[512,256]{1,0:T(8,128)S(1)}, ...), condition=%wide.region_4.5_spmd.clone, body=%wide.region_3.4_spmd.clone.sunk | while | flops 274465280 | bytes 1628365 | solution.py:57
  287.2 2.4 convolution_add_fusion.5
  289.8 2.4 convolution_add_fusion.5
  292.3 2.4 convolution_add_fusion.5
  294.8 2.4 convolution_add_fusion.5
  297.4 2.4 convolution_add_fusion.5
  300.0 2.4 convolution_add_fusion.5
  302.5 2.4 convolution_add_fusion.5
  305.0 2.4 convolution_add_fusion.5
  315.2 2.4 convolution_add_fusion.5
  317.8 2.4 convolution_add_fusion.5
  320.3 2.4 convolution_add_fusion.5
  322.9 2.4 convolution_add_fusion.5
  325.4 2.4 convolution_add_fusion.5
  327.9 2.4 convolution_add_fusion.5
  333.0 2.4 convolution_add_fusion.5
  335.6 2.4 convolution_add_fusion.5
  338.1 2.4 convolution_add_fusion.5
  348.3 2.4 convolution_add_fusion.5
  350.9 2.4 convolution_add_fusion.5
  355.9 2.4 convolution_add_fusion.5
  358.5 2.4 convolution_add_fusion.5
  370.5 24.1 %all-reduce.6.cloned.1.call-done = (f32[256,256]{1,0:T(8,128)}, f32[256,256]{1,0:T(8,128)}) async-done(((f32[256,256]{1,0:T(8,128)}, f32[256,256]{1,0:T(8,128)}), (f32[256,256]{1,0:T(8,128)}, f32[256,256]{1,0:T(8,128)})) %all-reduce.6.cloned.1.call-update) | async-done | bytes 524304 | tf_op jit(solution)/shard_map/psum | solution.py:65
  396.4 107.4 %all-gather.9.cloned.1.call-done = f32[32768,256]{1,0:T(8,128)} async-done(((f32[256,256]{1,0:T(8,128)}), f32[32768,256]{1,0:T(8,128)}) %all-gather.9.cloned.1.call-update) | async-done | bytes 33554448 | tf_op jit(solution)/shard_map/all_gather | solution.py:66
  503.8 12.0 %reduce_sum.9 = f32[256,256]{1,0:T(8,128)S(1)} reduce(f32[128,256,256]{2,1,0:T(8,128)} %bitcast.47, f32[]{:T(128)} %constant.95.clone.1), dimensions={0}, to_apply=%region_7.8 | reduce | flops 8323072 | bytes 33816580 | tf_op jit(solution)/shard_map/reduce_sum | solution.py:66
  (207 shorter events, 136.3 us)
Async XLA Ops:
  7.2 60.3 %all-gather.5.cloned.1.call-start = ((), (), s32[]{:S(2)}) async-start(), calls=%async_computation | async-start | bytes 8650752 | tf_op jit(solution)/shard_map/all_gather | solution.py:32
  9.7 198.7 %all-reduce.4.cloned.1.call-start = ((), (), s32[]{:S(2)}) async-start(), calls=%async_computation.1 | async-start | bytes 2097152 | tf_op jit(solution)/shard_map/psum | solution.py:44
  67.5 98.1 %copy-start.4 = (bf16[1024,256]{1,0:T(8,128)(2,1)S(1)}, bf16[1024,256]{1,0:T(8,128)(2,1)}, u32[]{:S(2)}) copy-start(bf16[1024,256]{1,0:T(8,128)(2,1)} %param.14) | copy-start | bytes 1572868
  163.9 1.0 copy-start.3
  163.9 2.8 copy-start.5
  164.9 122.2 %all-gather.7.cloned.1.call-start = ((), (), s32[]{:S(2)}) async-start(), calls=%async_computation.2 | async-start | bytes 17301504 | tf_op jit(solution)/shard_map/all_gather | solution.py:47
  166.6 43.2 %copy-start.2 = (bf16[1024,256]{1,0:T(8,128)(2,1)S(1)}, bf16[1024,256]{1,0:T(8,128)(2,1)}, u32[]{:S(2)}) copy-start(bf16[1024,256]{1,0:T(8,128)(2,1)} %broadcast_select_fusion) | copy-start | bytes 1572868
  166.6 227.9 %all-reduce.6.cloned.1.call-start = ((), (), s32[]{:S(2)}) async-start(), calls=%async_computation.4 | async-start | bytes 1048576 | tf_op jit(solution)/shard_map/psum | solution.py:65
  209.8 4.1 copy-start
  209.9 77.3 %copy-start.6 = (f32[3,512]{1,0:T(4,128)S(1)}, f32[3,512]{1,0:T(4,128)}, u32[]{:S(2)}) copy-start(f32[3,512]{1,0:T(4,128)} %param.11) | copy-start | bytes 18436
  214.0 289.8 %all-gather.9.cloned.1.call-start = ((), (), s32[]{:S(2)}) async-start(), calls=%async_computation.3 | async-start | bytes 33816576 | tf_op jit(solution)/shard_map/all_gather | solution.py:66
  368.7 147.1 %copy-start.1 = (f32[512,256]{1,0:T(8,128)}, f32[512,256]{1,0:T(8,128)S(1)}, u32[]{:S(2)}) copy-start(f32[512,256]{1,0:T(8,128)S(1)} %multiply_select_fusion.1) | copy-start | bytes 1572868
Sparse Core Ops, SparseCore 0:
  10.8 56.6 all-gather.4
  165.0 43.3 all-reduce.3
  211.2 75.8 all-gather.6
  290.8 103.6 all-reduce.5
  397.5 106.2 all-gather.8
